TPU v7x, 256 devices: a whole 4x4x8 slice. The times are simulated.
256 devices in a mesh: client: 32 (over z_lo, y, core), mp: 8 (over x, z_hi).
Axes of the slice: x: 4, y: 4, z: 8 (z_hi: 2, z_lo: 4; z = z_hi * 4 + z_lo), core: 2. Of those that a mesh axis runs over, the one named last changes fastest.
Arguments:
- hidden: bfloat16 [32, 4, 128, 7168], P('client', None, None, 'mp'), may hold values from -6 to 6
- weight: bfloat16 [32, 7168, 2048], P('client', 'mp'), may hold values from -0.0625 to 0.0625
- target: bfloat16 [32, 4, 128, 2048], P('client', None, 'mp'), may hold values from -6 to 6
- router_prob: float32 [32, 4, 128], P('client', None, 'mp'), may hold values from 0.2 to 1
- routes: int32 [32, 4, 128, 2], P('client', None, 'mp'), may hold values from 0 to 7, all different within a row
- assign: int32 [32, 1], replicated, may hold values from 0 to 3
Outputs:
- merged_weight: bfloat16 [32, 7168, 2048], P('client', 'mp')
Inputs may be any that keep to these rules, and one draw needn't show every extreme that they name: `routes`: each token names two different experts; the given weights are those of expert 0. `assign`: every cluster has at least one client.
All inputs are finite; a program needn't handle non-finite values.
Results may differ from a plain program's by a relative error of at most 0.0044.
The roundings to bfloat16 on the way count: a program that leaves them out, or rounds other values in their place, can miss the bound.
Values may be sent and summed in bfloat16 or wider, within the bound.
A program may use at most 128 MiB of HBM per device.

v0:
```python
import jax
import jax.numpy as jnp
from jax import lax
from jax.sharding import PartitionSpec as P

D = 2048
FFW = 7168
NB = 4
CLUSTERS = 4
EPS = 1e-06
FLOOR = 0.1


def body(hidden, weight, target, router_prob, routes, assign):
    local_weight = weight[0]
    fisher = jnp.zeros(local_weight.shape, jnp.float32)
    for batch in range(NB):
        batch_hidden = hidden[0, batch]
        outputs = lax.psum_scatter(
            jnp.dot(batch_hidden, local_weight, preferred_element_type=jnp.float32),
            "mp",
            scatter_dimension=0,
            tiled=True,
        )
        token_weight = jnp.where(
            jnp.any(routes[0, batch] == 0, axis=-1), router_prob[0, batch], 0.0
        )
        grad_out = (
            token_weight[:, None] * (outputs - target[0, batch].astype(jnp.float32))
        ).astype(jnp.bfloat16)
        grad = lax.dot_general(
            batch_hidden,
            lax.all_gather(grad_out, "mp", axis=0, tiled=True),
            (((0,), (0,)), ((), ())),
            preferred_element_type=jnp.float32,
        )
        fisher = fisher + grad * grad
    total_fisher = lax.psum(jnp.sum(fisher), "mp")
    mean_fisher = total_fisher / (FFW * D)
    a_weight = (fisher / (mean_fisher + EPS) + FLOOR).astype(jnp.bfloat16)
    got_a, got_w = (
        lax.all_to_all(a_weight[None], "client", split_axis=1, concat_axis=0, tiled=True),
        lax.all_to_all(local_weight[None], "client", split_axis=1, concat_axis=0, tiled=True),
    )
    member_table = (assign[:, 0][:, None] == jnp.arange(CLUSTERS)[None, :]).astype(jnp.float32)
    a_float = got_a.astype(jnp.float32)
    weighted = a_float * got_w.astype(jnp.float32)
    num_part = jnp.einsum("sk,srd->krd", member_table, weighted, precision=lax.Precision.HIGHEST)
    den_part = jnp.einsum("sk,srd->krd", member_table, a_float, precision=lax.Precision.HIGHEST)
    merged = (num_part / den_part).astype(jnp.bfloat16)
    own_cluster = lax.dynamic_index_in_dim(
        assign[:, 0], lax.axis_index("client"), 0, keepdims=False
    )
    every_cluster = lax.all_gather(merged, "client", axis=1, tiled=True)
    result = lax.dynamic_index_in_dim(every_cluster, own_cluster, 0, keepdims=True)
    return result


def solution(mesh):
    placed = (
        P("client", None, None, "mp"),
        P("client", "mp", None),
        P("client", None, "mp", None),
        P("client", None, "mp"),
        P("client", None, "mp", None),
        P(),
    )
    return jax.shard_map(
        body, mesh=mesh, in_specs=placed, out_specs=P("client", "mp", None), check_vma=False
    )
```

profile of v0, /device:TPU:1, one launch (start us, length us, event | category | flops | bytes accessed | tf_op | source)
XLA Modules:
  0.0 917.2 jit_solution(14706498457414140986)
XLA Ops:
  6.5 0.0 copy-start.1
  6.5 0.0 reduce-scatter.11.cloned.1.call-start
  6.5 3.9 fusion.2
  10.5 0.0 reduce-scatter.11.cloned.1.call-update
  10.5 0.0 reduce-scatter.5.cloned.1.call-start
  10.5 3.9 fusion.8
  14.4 0.0 reduce-scatter.5.cloned.1.call-update
  14.5 0.0 reduce-scatter.7.cloned.1.call-start
  14.5 0.0 copy-done.1
  14.5 3.8 fusion.6
  18.3 0.0 reduce-scatter.7.cloned.1.call-update
  18.3 7.8 copy.31
  26.1 0.6 broadcast.41
  26.7 23.7 %reduce.10 = bf16[896,2048]{1,0:T(8,128)(2,1)} reduce(bf16[896,1,2048]{2,1,0:T(2,128)(2,1)} %bitcast.73, bf16[]{:T(256)} %broadcast.41), dimensions={1}, to_apply=%bitcast.72.reduce_sub_computation | reduce | bytes 7340034
  50.3 8.7 reshape.64
  59.1 0.0 copy-start.3
  59.1 0.0 copy-start.5
  59.1 10.4 %all-to-all-start.1 = ((bf16[32,2,28672]{2,1,0:T(2,128)(2,1)}), bf16[32,2,28672]{2,1,0:T(2,128)(2,1)}, u32[]{:S(2)}, u32[]{:S(2)}) async-start(bf16[32,2,28672]{2,1,0:T(2,128)(2,1)} %reshape.64), calls=%async_computation.5 | async-start | bytes 7340032 | tf_op jit(solution)/shard_map/all_to_all | solution.py:43
  69.4 0.0 reduce-scatter.9.cloned.1.call-start
  69.5 3.7 fusion.4
  73.2 0.0 reduce-scatter.9.cloned.1.call-update
  73.3 0.0 copy-done.3
  73.3 0.0 copy-done.5
  73.3 27.6 %reduce-scatter.11.cloned.1.call-done = f32[16,2048]{1,0:T(8,128)} async-done(((f32[128,2048]{1,0:T(8,128)}), f32[16,2048]{1,0:T(8,128)}) %reduce-scatter.11.cloned.1.call-update) | async-done | bytes 131088 | tf_op jit(solution)/shard_map/reduce_scatter | solution.py:19
  100.9 95.0 %reduce-scatter.5.cloned.1.call-done = f32[16,2048]{1,0:T(8,128)} async-done(((f32[128,2048]{1,0:T(8,128)}), f32[16,2048]{1,0:T(8,128)}) %reduce-scatter.5.cloned.1.call-update) | async-done | bytes 131088 | tf_op jit(solution)/shard_map/reduce_scatter | solution.py:19
  195.9 86.6 %reduce-scatter.7.cloned.1.call-done = f32[16,2048]{1,0:T(8,128)} async-done(((f32[128,2048]{1,0:T(8,128)}), f32[16,2048]{1,0:T(8,128)}) %reduce-scatter.7.cloned.1.call-update) | async-done | bytes 131088 | tf_op jit(solution)/shard_map/reduce_scatter | solution.py:19
  282.5 87.1 %reduce-scatter.9.cloned.1.call-done = f32[16,2048]{1,0:T(8,128)} async-done(((f32[128,2048]{1,0:T(8,128)}), f32[16,2048]{1,0:T(8,128)}) %reduce-scatter.9.cloned.1.call-update) | async-done | bytes 131088 | tf_op jit(solution)/shard_map/reduce_scatter | solution.py:19
  369.7 0.0 copy-done.2
  369.7 1.2 fusion.39
  370.9 41.3 %all_gather.17 = bf16[128,2048]{1,0:T(8,128)(2,1)S(1)} all-gather(bf16[16,2048]{1,0:T(8,128)(2,1)S(1)} %get-tuple-element.12), channel_id=1, replica_groups=mesh['client'=32,'mp'=8] {'mp'}, dimensions={0}, use_global_device_ids=true | all-gather | bytes 589824 | tf_op jit(solution)/shard_map/all_gather | solution.py:33
  412.1 42.5 %all_gather.16 = bf16[128,2048]{1,0:T(8,128)(2,1)S(1)} all-gather(bf16[16,2048]{1,0:T(8,128)(2,1)S(1)} %get-tuple-element.10), channel_id=1, replica_groups=mesh['client'=32,'mp'=8] {'mp'}, dimensions={0}, use_global_device_ids=true | all-gather | bytes 589824 | tf_op jit(solution)/shard_map/all_gather | solution.py:33
  454.6 42.9 %all_gather.15 = bf16[128,2048]{1,0:T(8,128)(2,1)S(1)} all-gather(bf16[16,2048]{1,0:T(8,128)(2,1)S(1)} %get-tuple-element.11), channel_id=1, replica_groups=mesh['client'=32,'mp'=8] {'mp'}, dimensions={0}, use_global_device_ids=true | all-gather | bytes 589824 | tf_op jit(solution)/shard_map/all_gather | solution.py:33
  497.5 41.5 %all_gather.18 = bf16[128,2048]{1,0:T(8,128)(2,1)S(1)} all-gather(bf16[16,2048]{1,0:T(8,128)(2,1)S(1)} %get-tuple-element.9), channel_id=1, replica_groups=mesh['client'=32,'mp'=8] {'mp'}, dimensions={0}, use_global_device_ids=true | all-gather | bytes 589824 | tf_op jit(solution)/shard_map/all_gather | solution.py:33
  539.0 1.1 fusion.21
  540.2 1.1 fusion.24
  541.3 1.1 fusion.27
  542.5 4.9 fusion.51
  547.3 21.0 %psum.7 = f32[]{:T(128)} all-reduce(f32[]{:T(128)} %get-tuple-element.17), channel_id=1, replica_groups=mesh['client'=32,'mp'=8] {'mp'}, use_global_device_ids=true, to_apply=%region_9.10 | all-reduce | flops 1 | bytes 8 | tf_op jit(solution)/shard_map/psum | solution.py:38
  569.0 5.7 fusion.12
  574.7 18.1 %copy.15 = bf16[1,896,2048]{2,0,1:T(2,128)(2,1)} copy(bf16[1,896,2048]{1,2,0:T(8,128)(2,1)} %fusion.12) | data formatting | bytes 7340032 | tf_op jit(solution)/shard_map/broadcast_in_dim | solution.py:42
  592.8 23.7 %reduce.9 = bf16[896,2048]{1,0:T(8,128)(2,1)} reduce(bf16[896,1,2048]{2,1,0:T(2,128)(2,1)} %bitcast.74, bf16[]{:T(256)} %broadcast.41), dimensions={1}, to_apply=%bitcast.59.reduce_sub_computation | reduce | bytes 7340034
  616.5 8.7 reshape.62
  625.2 0.0 all-to-all-done.1
  625.2 38.2 %all-to-all-start = ((bf16[32,2,28672]{2,1,0:T(2,128)(2,1)}), bf16[32,2,28672]{2,1,0:T(2,128)(2,1)}, u32[]{:S(2)}, u32[]{:S(2)}) async-start(bf16[32,2,28672]{2,1,0:T(2,128)(2,1)} %reshape.62), calls=%async_computation.4 | async-start | bytes 7340032 | tf_op jit(solution)/shard_map/all_to_all | solution.py:42
  663.4 0.0 all-gather.2.cloned.1.call-start
  663.4 19.3 %reshape.65 = bf16[896,1,2048]{2,1,0:T(2,128)(2,1)} reshape(bf16[32,2,28672]{2,1,0:T(2,128)(2,1)} %all-to-all-done.1) | data formatting | bytes 7340032
  682.7 24.4 %convert_reduce_fusion = f32[896,2048]{1,0:T(8,128)} fusion(bf16[896,1,2048]{2,1,0:T(2,128)(2,1)} %reshape.65), kind=kLoop, calls=%fused_computation.4 | loop fusion | flops 1835008 | bytes 11010048 | tf_op jit(solution)/shard_map/convert_element_type | solution.py:47
  707.1 8.0 reshape.58
  715.1 30.2 %all-to-all-done = bf16[32,2,28672]{2,1,0:T(2,128)(2,1)} async-done(((bf16[32,2,28672]{2,1,0:T(2,128)(2,1)}), bf16[32,2,28672]{2,1,0:T(2,128)(2,1)}, u32[]{:S(2)}, u32[]{:S(2)}) %all-to-all-start) | async-done | bytes 3670048 | tf_op jit(solution)/shard_map/all_to_all | solution.py:42
  745.3 19.3 %reshape.63 = bf16[896,1,2048]{2,1,0:T(2,128)(2,1)} reshape(bf16[32,2,28672]{2,1,0:T(2,128)(2,1)} %all-to-all-done) | data formatting | bytes 7340032
  764.6 23.6 %bitcast_reduce_fusion = bf16[896,2048]{1,0:T(8,128)(2,1)} fusion(bf16[896,1,2048]{2,1,0:T(2,128)(2,1)} %reshape.63), kind=kLoop, calls=%fused_computation.65 | loop fusion | bytes 7340032 | tf_op jit(solution)/shard_map/all_to_all | solution.py:42
  788.2 5.9 all_to_all.7
  794.1 0.0 copy-start
  794.1 0.0 copy-start.4
  794.1 6.0 convert_multiply_fusion
  800.1 0.0 copy-done
  800.1 0.0 copy-done.4
  800.2 4.0 fusion.10
  804.2 7.7 fusion.16
  811.9 0.0 all-gather.2.cloned.1.call-update
  811.9 0.6 constant_dynamic-slice_fusion.1
  814.5 82.3 %all-gather.2.cloned.1.call-done = bf16[4,896,2048]{2,0,1:T(4,128)(2,1)} async-done(((bf16[4,28,2048]{2,0,1:T(4,128)(2,1)}), bf16[4,896,2048]{2,0,1:T(4,128)(2,1)}) %all-gather.2.cloned.1.call-update) | async-done | bytes 14680080 | tf_op jit(solution)/shard_map/all_gather | solution.py:54
  896.8 9.3 %constant_dynamic-slice_fusion = bf16[1,896,2048]{2,0,1:T(2,128)(2,1)S(1)} fusion(bf16[4,896,2048]{2,0,1:T(4,128)(2,1)} %all-gather.2.cloned.1.call-done, s32[]{:T(128)S(6)} %select_n.42), kind=kLoop, calls=%fused_computation.62 | loop fusion | bytes 7340036 | tf_op jit(solution)/shard_map/jit(dynamic_index_in_dim)/dynamic_slice | solution.py:55
  906.1 4.1 copy.19
  (3 shorter events, 0.0 us)
Async XLA Ops:
  6.5 8.0 copy-start.1
  6.5 94.4 %reduce-scatter.11.cloned.1.call-start = ((), (), s32[]{:S(2)}) async-start(), calls=%async_computation.9 | async-start | bytes 1179648 | tf_op jit(solution)/shard_map/reduce_scatter | solution.py:19
  10.5 185.4 %reduce-scatter.5.cloned.1.call-start = ((), (), s32[]{:S(2)}) async-start(), calls=%async_computation.6 | async-start | bytes 1179648 | tf_op jit(solution)/shard_map/reduce_scatter | solution.py:19
  14.5 268.1 %reduce-scatter.7.cloned.1.call-start = ((), (), s32[]{:S(2)}) async-start(), calls=%async_computation.7 | async-start | bytes 1179648 | tf_op jit(solution)/shard_map/reduce_scatter | solution.py:19
  59.1 14.2 %copy-start.3 = (s32[1,4,16,2]{2,3,1,0:T(2,128)S(1)}, s32[1,4,16,2]{2,3,1,0:T(2,128)}, u32[]{:S(2)}) copy-start(s32[1,4,16,2]{2,3,1,0:T(2,128)} %param.10) | copy-start | bytes 1540
  59.1 14.2 %copy-start.5 = (f32[1,4,16]{2,1,0:T(4,128)S(1)}, f32[1,4,16]{2,1,0:T(4,128)}, u32[]{:S(2)}) copy-start(f32[1,4,16]{2,1,0:T(4,128)} %param.9) | copy-start | bytes 772
  59.1 310.6 %copy-start.2 = (bf16[1,4,16,2048]{3,2,1,0:T(8,128)(2,1)S(1)}, bf16[1,4,16,2048]{3,2,1,0:T(8,128)(2,1)}, u32[]{:S(2)}) copy-start(bf16[1,4,16,2048]{3,2,1,0:T(8,128)(2,1)} %param.8) | copy-start | bytes 786436
  59.1 566.1 %all-to-all-start.1 = ((bf16[32,2,28672]{2,1,0:T(2,128)(2,1)}), bf16[32,2,28672]{2,1,0:T(2,128)(2,1)}, u32[]{:S(2)}, u32[]{:S(2)}) async-start(bf16[32,2,28672]{2,1,0:T(2,128)(2,1)} %reshape.64), calls=%async_computation.5 | async-start | bytes 7340032 | tf_op jit(solution)/shard_map/all_to_all | solution.py:43
  69.4 300.2 %reduce-scatter.9.cloned.1.call-start = ((), (), s32[]{:S(2)}) async-start(), calls=%async_computation.8 | async-start | bytes 1179648 | tf_op jit(solution)/shard_map/reduce_scatter | solution.py:19
  625.2 120.1 %all-to-all-start = ((bf16[32,2,28672]{2,1,0:T(2,128)(2,1)}), bf16[32,2,28672]{2,1,0:T(2,128)(2,1)}, u32[]{:S(2)}, u32[]{:S(2)}) async-start(bf16[32,2,28672]{2,1,0:T(2,128)(2,1)} %reshape.62), calls=%async_computation.4 | async-start | bytes 7340032 | tf_op jit(solution)/shard_map/all_to_all | solution.py:42
  663.4 233.5 %all-gather.2.cloned.1.call-start = ((), (), s32[]{:S(2)}) async-start(), calls=%async_computation.10 | async-start | bytes 15138816 | tf_op jit(solution)/shard_map/all_gather | solution.py:54
  794.1 6.0 copy-start
  794.1 6.0 copy-start.4
Sparse Core Ops, SparseCore 0:
  11.3 89.5 reduce-scatter.10
  105.3 90.5 reduce-scatter.4
  199.8 82.6 reduce-scatter.6
  286.8 82.7 reduce-scatter.8
  812.1 84.7 all-gather.1
where the time goes:
time: 926 us; the launch traced here: 917 us
  waiting for transfers between devices  409 us (44%)
  blocking collectives  189 us (20%)
  local copies, waits for them, and re-layouts  134 us (14%)
  other arithmetic  84.6 us (9%)
  starting transfers between devices  48.7 us (5%)
  matrix products  35.4 us (4%)
  between operations  16.3 us (2%)
    reduce_scatter x4, waiting for transfers between devices, body(): lax.psum_scatter(jnp.dot(batch_hidden, local_weight, preferred_element_ty...  296 us
    all_gather x4, blocking collectives, body(): lax.all_gather(grad_out, 'mp', axis=0, tiled=True)  168 us
    all_gather x1, waiting for transfers between devices, body(): every_cluster = lax.all_gather(merged, 'client', axis=1, tiled=True)  82.3 us
    unnamed x18, local copies, waits for them, and re-layouts  64.4 us
    unnamed x2, other arithmetic  47.4 us
    all_to_all x1, starting transfers between devices, body(): lax.all_to_all(a_weight[None], 'client', split_axis=1, concat_axis=0, til...  38.2 us
    all_to_all x1, waiting for transfers between devices, body(): lax.all_to_all(a_weight[None], 'client', split_axis=1, concat_axis=0, til...  30.2 us
    all_to_all x2, local copies, waits for them, and re-layouts, body(): lax.all_to_all(a_weight[None], 'client', split_axis=1, concat_axis=0, til...  29.5 us
  transfers between devices with their start and end apart: 7, of which 6 were waited for; matrix products, arithmetic and copies ran while one was open for 19% of the time, Pallas kernels for 0%

commit v1 on v0

--- a/solution.py
+++ b/solution.py
@@ -51,7 +51,9 @@
     own_cluster = lax.dynamic_index_in_dim(
         assign[:, 0], lax.axis_index("client"), 0, keepdims=False
     )
-    every_cluster = lax.all_gather(merged, "client", axis=1, tiled=True)
+    every_cluster = jnp.concatenate(
+        lax.all_to_all(jnp.stack(lax.axis_size("client") * [merged], axis=0), "client", 0, 0), 1
+    )
     result = lax.dynamic_index_in_dim(every_cluster, own_cluster, 0, keepdims=True)
     return result
 

time: 926 us -> 1180 us (1.27)
  waiting for transfers between devices: 409 us -> 650 us
    all_to_all x0 -> x1, waiting for transfers between devices: none -> 324 us  [body(): lax.all_to_all(jnp.stack(lax.axis_size('client') * [merged], axis=0), 'cl...]
    all_gather x1 -> x0, waiting for transfers between devices: 82.3 us -> none  [body(): every_cluster = lax.all_gather(merged, 'client', axis=1, tiled=True)]
  transfers between devices with their start and end apart: 7 -> 7, of which waited for: 6 -> 6; matrix products, arithmetic and copies ran while one was open for 19% -> 15% of each run, Pallas kernels for 0% -> 0%
where the time goes in v1:
time: 1180 us; the launch traced here: 1170 us
  waiting for transfers between devices  650 us (55%)
  blocking collectives  189 us (16%)
  local copies, waits for them, and re-layouts  142 us (12%)
  other arithmetic  84.6 us (7%)
  starting transfers between devices  55.3 us (5%)
  matrix products  34.6 us (3%)
  between operations  16.3 us (1%)
    all_to_all x1, waiting for transfers between devices, body(): lax.all_to_all(jnp.stack(lax.axis_size('client') * [merged], axis=0), 'cl...  324 us
    reduce_scatter x4, waiting for transfers between devices, body(): lax.psum_scatter(jnp.dot(batch_hidden, local_weight, preferred_element_ty...  296 us
    all_gather x4, blocking collectives, body(): lax.all_gather(grad_out, 'mp', axis=0, tiled=True)  168 us
    unnamed x18, local copies, waits for them, and re-layouts  64.4 us
    unnamed x2, other arithmetic  47.4 us
    all_to_all x1, starting transfers between devices, body(): lax.all_to_all(a_weight[None], 'client', split_axis=1, concat_axis=0, til...  38.2 us
    all_to_all x1, waiting for transfers between devices, body(): lax.all_to_all(a_weight[None], 'client', split_axis=1, concat_axis=0, til...  30.2 us
    all_to_all x2, local copies, waits for them, and re-layouts, body(): lax.all_to_all(a_weight[None], 'client', split_axis=1, concat_axis=0, til...  29.5 us
  transfers between devices with their start and end apart: 7, of which 6 were waited for; matrix products, arithmetic and copies ran while one was open for 15% of the time, Pallas kernels for 0%

profile of v1, /device:TPU:1, one launch (start us, length us, event | category | flops | bytes accessed | tf_op | source)
XLA Modules:
  0.0 1172.5 jit_solution(10727283459516548430)
XLA Ops:
  6.5 0.0 copy-start.1
  6.5 0.0 reduce-scatter.11.cloned.1.call-start
  6.5 3.9 fusion.2
  10.5 0.0 reduce-scatter.11.cloned.1.call-update
  10.5 0.0 reduce-scatter.5.cloned.1.call-start
  10.5 3.9 fusion.8
  14.4 0.0 reduce-scatter.5.cloned.1.call-update
  14.5 0.0 reduce-scatter.7.cloned.1.call-start
  14.5 0.0 copy-done.1
  14.5 3.8 fusion.6
  18.3 0.0 reduce-scatter.7.cloned.1.call-update
  18.3 7.8 copy.31
  26.1 0.6 broadcast.43
  26.7 23.7 %reduce.10 = bf16[896,2048]{1,0:T(8,128)(2,1)} reduce(bf16[896,1,2048]{2,1,0:T(2,128)(2,1)} %bitcast.76, bf16[]{:T(256)} %broadcast.43), dimensions={1}, to_apply=%bitcast.75.reduce_sub_computation | reduce | bytes 7340034
  50.3 8.7 reshape.74
  59.1 0.0 copy-start.3
  59.1 0.0 copy-start.5
  59.1 10.4 all-to-all-start.1
  69.4 0.0 reduce-scatter.9.cloned.1.call-start
  69.5 3.7 fusion.4
  73.2 0.0 reduce-scatter.9.cloned.1.call-update
  73.3 0.0 copy-done.3
  73.3 0.0 copy-done.5
  73.3 27.6 %reduce-scatter.11.cloned.1.call-done = f32[16,2048]{1,0:T(8,128)} async-done(((f32[128,2048]{1,0:T(8,128)}), f32[16,2048]{1,0:T(8,128)}) %reduce-scatter.11.cloned.1.call-update) | async-done | bytes 131088 | tf_op jit(solution)/shard_map/reduce_scatter | solution.py:19
  100.9 95.0 %reduce-scatter.5.cloned.1.call-done = f32[16,2048]{1,0:T(8,128)} async-done(((f32[128,2048]{1,0:T(8,128)}), f32[16,2048]{1,0:T(8,128)}) %reduce-scatter.5.cloned.1.call-update) | async-done | bytes 131088 | tf_op jit(solution)/shard_map/reduce_scatter | solution.py:19
  195.9 86.6 %reduce-scatter.7.cloned.1.call-done = f32[16,2048]{1,0:T(8,128)} async-done(((f32[128,2048]{1,0:T(8,128)}), f32[16,2048]{1,0:T(8,128)}) %reduce-scatter.7.cloned.1.call-update) | async-done | bytes 131088 | tf_op jit(solution)/shard_map/reduce_scatter | solution.py:19
  282.5 87.1 %reduce-scatter.9.cloned.1.call-done = f32[16,2048]{1,0:T(8,128)} async-done(((f32[128,2048]{1,0:T(8,128)}), f32[16,2048]{1,0:T(8,128)}) %reduce-scatter.9.cloned.1.call-update) | async-done | bytes 131088 | tf_op jit(solution)/shard_map/reduce_scatter | solution.py:19
  369.7 0.0 copy-done.2
  369.7 1.2 fusion.39
  370.9 41.3 %all_gather.14 = bf16[128,2048]{1,0:T(8,128)(2,1)S(1)} all-gather(bf16[16,2048]{1,0:T(8,128)(2,1)S(1)} %get-tuple-element.12), channel_id=1, replica_groups=mesh['client'=32,'mp'=8] {'mp'}, dimensions={0}, use_global_device_ids=true | all-gather | bytes 589824 | tf_op jit(solution)/shard_map/all_gather | solution.py:33
  412.1 42.5 %all_gather.13 = bf16[128,2048]{1,0:T(8,128)(2,1)S(1)} all-gather(bf16[16,2048]{1,0:T(8,128)(2,1)S(1)} %get-tuple-element.10), channel_id=1, replica_groups=mesh['client'=32,'mp'=8] {'mp'}, dimensions={0}, use_global_device_ids=true | all-gather | bytes 589824 | tf_op jit(solution)/shard_map/all_gather | solution.py:33
  454.6 42.9 %all_gather.12 = bf16[128,2048]{1,0:T(8,128)(2,1)S(1)} all-gather(bf16[16,2048]{1,0:T(8,128)(2,1)S(1)} %get-tuple-element.11), channel_id=1, replica_groups=mesh['client'=32,'mp'=8] {'mp'}, dimensions={0}, use_global_device_ids=true | all-gather | bytes 589824 | tf_op jit(solution)/shard_map/all_gather | solution.py:33
  497.5 41.5 %all_gather.15 = bf16[128,2048]{1,0:T(8,128)(2,1)S(1)} all-gather(bf16[16,2048]{1,0:T(8,128)(2,1)S(1)} %get-tuple-element.9), channel_id=1, replica_groups=mesh['client'=32,'mp'=8] {'mp'}, dimensions={0}, use_global_device_ids=true | all-gather | bytes 589824 | tf_op jit(solution)/shard_map/all_gather | solution.py:33
  539.0 1.1 fusion.21
  540.2 1.1 fusion.24
  541.3 1.1 fusion.27
  542.5 4.9 fusion.51
  547.3 21.0 %psum.7 = f32[]{:T(128)} all-reduce(f32[]{:T(128)} %get-tuple-element.17), channel_id=1, replica_groups=mesh['client'=32,'mp'=8] {'mp'}, use_global_device_ids=true, to_apply=%region_9.10 | all-reduce | flops 1 | bytes 8 | tf_op jit(solution)/shard_map/psum | solution.py:38
  569.0 5.7 fusion.12
  574.7 18.1 %copy.15 = bf16[1,896,2048]{2,0,1:T(2,128)(2,1)} copy(bf16[1,896,2048]{1,2,0:T(8,128)(2,1)} %fusion.12) | data formatting | bytes 7340032 | tf_op jit(solution)/shard_map/broadcast_in_dim | solution.py:42
  592.8 23.7 %reduce.9 = bf16[896,2048]{1,0:T(8,128)(2,1)} reduce(bf16[896,1,2048]{2,1,0:T(2,128)(2,1)} %bitcast.77, bf16[]{:T(256)} %broadcast.43), dimensions={1}, to_apply=%bitcast.62.reduce_sub_computation | reduce | bytes 7340034
  616.5 8.7 reshape.72
  625.2 0.0 all-to-all-done.1
  625.2 38.2 %all-to-all-start = ((bf16[32,2,28672]{2,1,0:T(2,128)(2,1)}), bf16[32,2,28672]{2,1,0:T(2,128)(2,1)}, u32[]{:S(2)}, u32[]{:S(2)}) async-start(bf16[32,2,28672]{2,1,0:T(2,128)(2,1)} %reshape.72), calls=%async_computation.4 | async-start | bytes 7340032 | tf_op jit(solution)/shard_map/all_to_all | solution.py:42
  663.4 19.3 %reshape.75 = bf16[896,1,2048]{2,1,0:T(2,128)(2,1)} reshape(bf16[32,2,28672]{2,1,0:T(2,128)(2,1)} %all-to-all-done.1) | data formatting | bytes 7340032
  682.7 24.4 %convert_reduce_fusion = f32[896,2048]{1,0:T(8,128)} fusion(bf16[896,1,2048]{2,1,0:T(2,128)(2,1)} %reshape.75), kind=kLoop, calls=%fused_computation.4 | loop fusion | flops 1835008 | bytes 11010048 | tf_op jit(solution)/shard_map/convert_element_type | solution.py:47
  707.1 8.0 reshape.68
  715.1 30.2 %all-to-all-done = bf16[32,2,28672]{2,1,0:T(2,128)(2,1)} async-done(((bf16[32,2,28672]{2,1,0:T(2,128)(2,1)}), bf16[32,2,28672]{2,1,0:T(2,128)(2,1)}, u32[]{:S(2)}, u32[]{:S(2)}) %all-to-all-start) | async-done | bytes 3670048 | tf_op jit(solution)/shard_map/all_to_all | solution.py:42
  745.3 19.3 %reshape.73 = bf16[896,1,2048]{2,1,0:T(2,128)(2,1)} reshape(bf16[32,2,28672]{2,1,0:T(2,128)(2,1)} %all-to-all-done) | data formatting | bytes 7340032
  764.6 23.6 %bitcast_reduce_fusion = bf16[896,2048]{1,0:T(8,128)(2,1)} fusion(bf16[896,1,2048]{2,1,0:T(2,128)(2,1)} %reshape.73), kind=kLoop, calls=%fused_computation.65 | loop fusion | bytes 7340032 | tf_op jit(solution)/shard_map/all_to_all | solution.py:42
  788.2 5.9 all_to_all.9
  794.1 0.0 copy-start
  794.1 0.0 copy-start.4
  794.1 6.0 convert_multiply_fusion
  800.1 0.0 copy-done
  800.1 0.0 copy-done.4
  800.2 4.0 fusion.10
  804.2 7.0 fusion.16
  811.1 8.3 stack.2
  819.5 6.6 all-to-all-start.2
  826.1 0.6 constant_dynamic-slice_fusion.1
  828.6 323.5 %all-to-all-done.2 = bf16[32,4,28,2048]{3,1,2,0:T(4,128)(2,1)} async-done(((bf16[32,4,28,2048]{3,1,2,0:T(4,128)(2,1)}), bf16[32,4,28,2048]{3,1,2,0:T(4,128)(2,1)}, u32[]{:S(2)}, u32[]{:S(2)}) %all-to-all-start.2) | async-done | bytes 14680096 | tf_op jit(solution)/shard_map/all_to_all | solution.py:55
  1152.1 9.3 constant_dynamic-slice_fusion
  1161.4 4.1 copy.19
  (3 shorter events, 0.0 us)
Async XLA Ops:
  6.5 8.0 copy-start.1
  6.5 94.4 %reduce-scatter.11.cloned.1.call-start = ((), (), s32[]{:S(2)}) async-start(), calls=%async_computation.10 | async-start | bytes 1179648 | tf_op jit(solution)/shard_map/reduce_scatter | solution.py:19
  10.5 185.4 %reduce-scatter.5.cloned.1.call-start = ((), (), s32[]{:S(2)}) async-start(), calls=%async_computation.7 | async-start | bytes 1179648 | tf_op jit(solution)/shard_map/reduce_scatter | solution.py:19
  14.5 268.1 %reduce-scatter.7.cloned.1.call-start = ((), (), s32[]{:S(2)}) async-start(), calls=%async_computation.8 | async-start | bytes 1179648 | tf_op jit(solution)/shard_map/reduce_scatter | solution.py:19
  59.1 14.2 %copy-start.3 = (s32[1,4,16,2]{2,3,1,0:T(2,128)S(1)}, s32[1,4,16,2]{2,3,1,0:T(2,128)}, u32[]{:S(2)}) copy-start(s32[1,4,16,2]{2,3,1,0:T(2,128)} %param.10) | copy-start | bytes 1540
  59.1 14.2 %copy-start.5 = (f32[1,4,16]{2,1,0:T(4,128)S(1)}, f32[1,4,16]{2,1,0:T(4,128)}, u32[]{:S(2)}) copy-start(f32[1,4,16]{2,1,0:T(4,128)} %param.9) | copy-start | bytes 772
  59.1 310.6 %copy-start.2 = (bf16[1,4,16,2048]{3,2,1,0:T(8,128)(2,1)S(1)}, bf16[1,4,16,2048]{3,2,1,0:T(8,128)(2,1)}, u32[]{:S(2)}) copy-start(bf16[1,4,16,2048]{3,2,1,0:T(8,128)(2,1)} %param.8) | copy-start | bytes 786436
  59.1 566.1 %all-to-all-start.1 = ((bf16[32,2,28672]{2,1,0:T(2,128)(2,1)}), bf16[32,2,28672]{2,1,0:T(2,128)(2,1)}, u32[]{:S(2)}, u32[]{:S(2)}) async-start(bf16[32,2,28672]{2,1,0:T(2,128)(2,1)} %reshape.74), calls=%async_computation.5 | async-start | bytes 7340032 | tf_op jit(solution)/shard_map/all_to_all | solution.py:43
  69.4 300.2 %reduce-scatter.9.cloned.1.call-start = ((), (), s32[]{:S(2)}) async-start(), calls=%async_computation.9 | async-start | bytes 1179648 | tf_op jit(solution)/shard_map/reduce_scatter | solution.py:19
  625.2 120.1 %all-to-all-start = ((bf16[32,2,28672]{2,1,0:T(2,128)(2,1)}), bf16[32,2,28672]{2,1,0:T(2,128)(2,1)}, u32[]{:S(2)}, u32[]{:S(2)}) async-start(bf16[32,2,28672]{2,1,0:T(2,128)(2,1)} %reshape.72), calls=%async_computation.4 | async-start | bytes 7340032 | tf_op jit(solution)/shard_map/all_to_all | solution.py:42
  794.1 6.0 copy-start
  794.1 6.0 copy-start.4
  819.5 332.7 %all-to-all-start.2 = ((bf16[32,4,28,2048]{3,1,2,0:T(4,128)(2,1)}), bf16[32,4,28,2048]{3,1,2,0:T(4,128)(2,1)}, u32[]{:S(2)}, u32[]{:S(2)}) async-start(bf16[32,4,28,2048]{3,1,2,0:T(4,128)(2,1)} %stack.2), calls=%async_computation.6 | async-start | bytes 29360128 | tf_op jit(solution)/shard_map/all_to_all | solution.py:55
Sparse Core Ops, SparseCore 0:
  11.3 89.5 reduce-scatter.10
  105.3 90.5 reduce-scatter.4
  199.8 82.6 reduce-scatter.6
  286.8 82.7 reduce-scatter.8
